TPU v7x, 128 devices: a whole 4x4x4 slice. The times are simulated.
128 devices in a mesh: rows: 32 (over x, y, z_lo), feat: 4 (over z_hi, core).
Axes of the slice: x: 4, y: 4, z: 4 (z_hi: 2, z_lo: 2; z = z_hi * 2 + z_lo), core: 2. Of those that a mesh axis runs over, the one named last changes fastest.
Arguments:
- node_feats: bfloat16 [256, 131072], P('feat', 'rows'), may hold values from -6 to 6
- tile_vals: bfloat16 [1024, 16, 128, 128], P('rows'), may hold values from -0.125 to 0.125
- tile_cols: int32 [1024, 16], P('rows'), may hold values from 0 to 1023, as said below
- weight: bfloat16 [256, 256], P(None, 'feat'), may hold values from -0.375 to 0.375
- bias_vec: float32 [256], P('feat'), may hold values from -3 to 3
- grad_out: bfloat16 [256, 131072], P('feat', 'rows'), may hold values from -6 to 6
Outputs:
- activated: bfloat16 [256, 131072], P('feat', 'rows')
- grad_feats: float32 [256, 131072], P('feat', 'rows')
- grad_weight: float32 [256, 256], P(None, 'feat')
- grad_bias: float32 [256], P('feat')
Inputs may be any that keep to these rules, and one draw needn't show every extreme that they name: `tile_cols`: among the tiles of one device's 32 blocks of rows, the column blocks held by any one owner (blocks o * 32 to o * 32 + 31) are at most 16 distinct ones and at least one; on every device some owner reaches 16.
All inputs are finite; a program needn't handle non-finite values.
Results may differ from a plain program's by a relative error of at most 0.007.
Values may be sent and summed in bfloat16 or wider, within the bound.
No kernel may reach another device: no remote copies, remote signals or barrier semaphores. Data moves between devices by JAX's collectives and lax.ppermute only.
A program may use at most 256 MiB of HBM per device.

v0:
```python
import jax
import jax.numpy as jnp
from jax import lax
from jax.sharding import PartitionSpec as P


def on_device(node_feats, tile_vals, tile_cols, weight, bias_vec, grad_out):
    feat_loc = node_feats.shape[0]
    own_blocks = tile_cols.shape[0]
    slots_per = tile_cols.shape[1]
    tile_edge = tile_vals.shape[2]
    row_devs = lax.axis_size("rows")
    flat_cols = tile_cols.reshape(-1)
    whole = lax.all_gather(node_feats, "rows", axis=1, tiled=True)
    picked = jnp.take(whole.reshape(feat_loc, -1, tile_edge), flat_cols, axis=1)
    picked = picked.reshape(feat_loc, own_blocks, slots_per, tile_edge)
    aggregated = jnp.einsum("fisb,isab->fia", picked, tile_vals, preferred_element_type=jnp.float32)
    aggregated = aggregated.reshape(feat_loc, own_blocks * tile_edge).astype(jnp.bfloat16)
    agg_all = lax.all_gather(aggregated, "feat", axis=0, tiled=True)
    preact = (
        lax.dot_general(
            weight, agg_all, (((0,), (0,)), ((), ())), preferred_element_type=jnp.float32
        )
        + bias_vec[:, None]
    )
    sigma = jax.nn.sigmoid(preact)
    activated = (preact * sigma).astype(jnp.bfloat16)
    grad_pre = (grad_out.astype(jnp.float32) * sigma * (1.0 + preact * (1.0 - sigma))).astype(
        jnp.bfloat16
    )
    weight_part = lax.dot_general(
        agg_all, grad_pre, (((1,), (1,)), ((), ())), preferred_element_type=jnp.float32
    )
    bias_part = jnp.sum(grad_pre.astype(jnp.float32), axis=1)
    grad_weight, grad_bias = lax.psum((weight_part, bias_part), "rows")
    back_mix = lax.psum_scatter(
        jnp.dot(weight, grad_pre, preferred_element_type=jnp.float32),
        "feat",
        scatter_dimension=0,
        tiled=True,
    )
    back_mix = back_mix.astype(jnp.bfloat16)
    contrib = jnp.einsum(
        "fia,isab->fisb",
        back_mix.reshape(feat_loc, own_blocks, tile_edge),
        tile_vals,
        preferred_element_type=jnp.float32,
    )
    contrib = contrib.reshape(feat_loc, own_blocks * slots_per, tile_edge)
    terms = (
        jnp.zeros((feat_loc, row_devs * own_blocks, tile_edge), jnp.float32)
        .at[:, flat_cols]
        .add(contrib)
    )
    grad_feats = lax.psum_scatter(
        terms.reshape(feat_loc, -1), "rows", scatter_dimension=1, tiled=True
    )
    return (activated, grad_feats, grad_weight, grad_bias)


def solution(mesh):
    placed = (
        P("feat", "rows"),
        P("rows", None, None, None),
        P("rows", None),
        P(None, "feat"),
        P("feat"),
        P("feat", "rows"),
    )
    return jax.shard_map(
        on_device,
        mesh=mesh,
        in_specs=placed,
        out_specs=(P("feat", "rows"), P("feat", "rows"), P(None, "feat"), P("feat")),
        check_vma=False,
    )
```

profile of v0, /device:TPU:1, one launch (start us, length us, event | category | flops | bytes accessed | tf_op | source)
XLA Modules:
  0.0 1509.5 jit_solution(4154071832402100049)
XLA Ops:
  7.2 0.0 copy-start
  7.2 0.0 all-gather.3.cloned.1.call-start
  7.2 0.7 all-gather.3.cloned.1.call-update
  7.9 0.0 all-gather.5.cloned.1.call-start
  8.0 0.8 copy.25
  8.7 0.7 compare_and_fusion
  9.4 0.1 copy.24
  9.5 0.1 reshape.64
  9.6 363.7 %all-gather.3.cloned.1.call-done = bf16[64,131072]{1,0:T(8,128)(2,1)} async-done(((bf16[64,4096]{1,0:T(8,128)(2,1)}), bf16[64,131072]{1,0:T(8,128)(2,1)}) %all-gather.3.cloned.1.call-update) | async-done | bytes 16777232 | tf_op jit(solution)/shard_map/all_gather | solution.py:14
  373.4 15.3 %copy_bitcast_fusion.1 = bf16[64,1024,128]{2,0,1:T(8,128)(2,1)} fusion(bf16[64,131072]{1,0:T(8,128)(2,1)} %all-gather.3.cloned.1.call-done), kind=kLoop, calls=%fused_computation.3 | loop fusion | bytes 33554432 | tf_op jit(solution)/shard_map/reshape | solution.py:15
  388.6 25.4 %gather_fusion = bf16[512,64,128]{2,1,0:T(8,128)(2,1)} fusion(bf16[64,1024,128]{2,0,1:T(8,128)(2,1)} %copy_bitcast_fusion.1, s32[1024]{0:T(1024)S(1)} %pad_clamp_fusion), kind=kCustom, calls=%fused_computation | custom fusion | bytes 16779264 | tf_op jit(solution)/shard_map/jit(_take)/gather | solution.py:15
  414.1 0.0 copy-start.3
  414.1 0.0 copy-start.4
  414.1 11.4 fusion.11
  425.5 0.9 copy.42
  426.4 0.0 all-gather.5.cloned.1.call-update
  426.4 0.0 reduce-scatter.7.cloned.1.call-start
  426.5 29.9 %all-gather.5.cloned.1.call-done = bf16[256,4096]{1,0:T(8,128)(2,1)} async-done(((bf16[64,4096]{1,0:T(8,128)(2,1)}), bf16[256,4096]{1,0:T(8,128)(2,1)}) %all-gather.5.cloned.1.call-update) | async-done | bytes 2097168 | tf_op jit(solution)/shard_map/all_gather | solution.py:19
  456.4 0.0 copy-done
  456.4 0.0 copy-done.3
  456.4 0.0 copy-done.4
  456.4 0.0 copy-start.2
  456.4 3.5 convert_reduce_fusion
  459.8 2.7 convolution_bitcast_fusion
  462.6 5.6 copy.34
  468.2 0.0 reduce-scatter.7.cloned.1.call-update
  468.2 0.0 all-reduce.2.cloned.1.call-start
  468.3 0.0 copy-done.2
  468.3 1.4 fusion.16
  469.7 0.0 all-reduce.2.cloned.1.call-update
  469.7 0.2 reduce-scatter.5.cloned.1.call-start
  469.9 48.8 %reduce-scatter.7.cloned.1.call-done = f32[64,4096]{1,0:T(8,128)} async-done(((f32[256,4096]{1,0:T(8,128)}), f32[64,4096]{1,0:T(8,128)}) %reduce-scatter.7.cloned.1.call-update) | async-done | bytes 1048592
  518.7 1.7 copy.35
  520.4 14.0 fusion.15
  534.4 11.3 broadcast_in_dim.17
  545.7 78.5 %scatter_fusion = f32[64,1024,128]{2,0,1:T(8,128)} fusion(f32[64,1024,128]{2,0,1:T(8,128)} %broadcast_in_dim.17, s32[512]{0:T(512)S(1)} %bitcast.56, f32[512,64,128]{2,1,0:T(8,128)} %bitcast.51), kind=kCustom, calls=%fused_computation.1 | custom fusion | flops 4194304 | bytes 50333696 | tf_op jit(solution)/shard_map/scatter-add | solution.py:53
  624.2 22.5 %copy_bitcast_fusion = f32[64,131072]{1,0:T(8,128)} fusion(f32[64,1024,128]{2,0,1:T(8,128)} %scatter_fusion), kind=kLoop, calls=%fused_computation.2 | loop fusion | bytes 67108864 | tf_op jit(solution)/shard_map/reshape | solution.py:56
  646.6 0.0 copy-start.1
  646.6 0.0 reduce-scatter.5.cloned.1.call-update
  646.7 68.7 %psum.15 = f32[64]{0:T(128)} all-reduce(f32[64]{0:T(128)S(1)} %get-tuple-element.4), channel_id=1, replica_groups=mesh['rows'=32,'feat'=4] {'rows'}, use_global_device_ids=true, to_apply=%region_5.6 | all-reduce | flops 64 | bytes 512 | tf_op jit(solution)/shard_map/psum | solution.py:35
  715.3 62.1 %all-reduce.2.cloned.1.call-done = f32[256,64]{0,1:T(8,128)} async-done(((f32[256,64]{0,1:T(8,128)}), f32[256,64]{0,1:T(8,128)}) %all-reduce.2.cloned.1.call-update) | async-done | bytes 65552 | tf_op jit(solution)/shard_map/psum | solution.py:35
  777.4 724.1 %reduce-scatter.5.cloned.1.call-done = f32[64,4096]{1,0:T(8,128)} async-done(((f32[64,131072]{1,0:T(8,128)}), f32[64,4096]{1,0:T(8,128)}) %reduce-scatter.5.cloned.1.call-update) | async-done | bytes 1048592 | tf_op jit(solution)/shard_map/reduce_scatter | solution.py:55
  1501.5 1.5 copy.45
  1503.0 0.0 copy-done.1
  (2 shorter events, 0.0 us)
Async XLA Ops:
  7.2 449.2 %copy-start = (bf16[256,64]{0,1:T(8,128)(2,1)S(1)}, bf16[256,64]{0,1:T(8,128)(2,1)}, u32[]{:S(2)}) copy-start(bf16[256,64]{0,1:T(8,128)(2,1)} %param.9) | copy-start | bytes 98308
  7.2 366.2 %all-gather.3.cloned.1.call-start = ((), (), s32[]{:S(2)}) async-start(), calls=%async_computation.2 | async-start | bytes 17301504 | tf_op jit(solution)/shard_map/all_gather | solution.py:14
  7.9 448.4 %all-gather.5.cloned.1.call-start = ((), (), s32[]{:S(2)}) async-start(), calls=%async_computation.3 | async-start | bytes 2621440 | tf_op jit(solution)/shard_map/all_gather | solution.py:19
  414.1 42.3 %copy-start.3 = (bf16[64,4096]{1,0:T(8,128)(2,1)S(1)}, bf16[64,4096]{1,0:T(8,128)(2,1)}, u32[]{:S(2)}) copy-start(bf16[64,4096]{1,0:T(8,128)(2,1)} %param.11) | copy-start | bytes 1572868
  414.1 42.3 %copy-start.4 = (f32[64]{0:T(128)S(1)}, f32[64]{0:T(128)}, u32[]{:S(2)}) copy-start(f32[64]{0:T(128)} %param.10) | copy-start | bytes 772
  426.4 92.3 %reduce-scatter.7.cloned.1.call-start = ((), (), s32[]{:S(2)}) async-start(), calls=%async_computation.6 | async-start | bytes 5242880
  456.4 11.9 copy-start.2
  468.2 309.2 %all-reduce.2.cloned.1.call-start = ((), (), s32[]{:S(2)}) async-start(), calls=%async_computation.5 | async-start | bytes 131072 | tf_op jit(solution)/shard_map/psum | solution.py:35
  469.7 1031.8 %reduce-scatter.5.cloned.1.call-start = ((), (), s32[]{:S(2)}) async-start(), calls=%async_computation.4 | async-start | bytes 34603008 | tf_op jit(solution)/shard_map/reduce_scatter | solution.py:55
  646.6 856.4 %copy-start.1 = (bf16[256,64]{0,1:T(8,128)(2,1)S(1)}, bf16[256,64]{0,1:T(8,128)(2,1)}, u32[]{:S(2)}) copy-start(bf16[256,64]{0,1:T(8,128)(2,1)} %param.9) | copy-start | bytes 98308
Sparse Core Ops, SparseCore 0:
  9.7 363.6 all-gather.2
  426.6 29.7 all-gather.4
  468.4 50.3 reduce-scatter.6
  521.8 255.5 all-reduce.1
  780.2 721.2 reduce-scatter.4
where the time goes:
time: 1510 us
  waiting for transfers between devices  1230 us (81%)
  local copies, waits for them, and re-layouts  85.1 us (6%)
  other arithmetic  79.2 us (5%)
  blocking collectives  68.7 us (5%)
  matrix products  33 us (2%)
    reduce_scatter x1, waiting for transfers between devices, on_device(): lax.psum_scatter(terms.reshape(feat_loc, -1), 'rows', scatter_dimension=1...  724 us
    all_gather x1, waiting for transfers between devices, on_device(): whole = lax.all_gather(node_feats, 'rows', axis=1, tiled=True)  364 us
    scatter-add x1, other arithmetic, on_device(): terms = jnp.zeros((feat_loc, row_devs * own_blocks, tile_edge), jnp.float...  78.5 us
    psum x1, blocking collectives, on_device(): grad_weight, grad_bias = lax.psum((weight_part, bias_part), 'rows')  68.7 us
    psum x1, waiting for transfers between devices, on_device(): grad_weight, grad_bias = lax.psum((weight_part, bias_part), 'rows')  62.1 us
    unnamed x6, waiting for transfers between devices  49.5 us
  transfers between devices with their start and end apart: 5, of which 5 were waited for; matrix products, arithmetic and copies ran while one was open for 9% of the time, Pallas kernels for 0%

commit v1 on v0

--- a/solution.py
+++ b/solution.py
@@ -11,7 +11,9 @@
     tile_edge = tile_vals.shape[2]
     row_devs = lax.axis_size("rows")
     flat_cols = tile_cols.reshape(-1)
-    whole = lax.all_gather(node_feats, "rows", axis=1, tiled=True)
+    whole = jnp.concatenate(
+        lax.all_to_all(jnp.stack([node_feats] * lax.axis_size("rows")), "rows", 0, 0), axis=1
+    )
     picked = jnp.take(whole.reshape(feat_loc, -1, tile_edge), flat_cols, axis=1)
     picked = picked.reshape(feat_loc, own_blocks, slots_per, tile_edge)
     aggregated = jnp.einsum("fisb,isab->fia", picked, tile_vals, preferred_element_type=jnp.float32)

time: 1510 us -> 1570 us (1.040)
  local copies, waits for them, and re-layouts: 85.1 us -> 139 us
    all_gather x1 -> x0, waiting for transfers between devices: 364 us -> none  [on_device(): whole = lax.all_gather(node_feats, 'rows', axis=1, tiled=True)]
    all_to_all x0 -> x1, waiting for transfers between devices: none -> 340 us  [on_device(): lax.all_to_all(jnp.stack([node_feats] * lax.axis_size('rows')), 'rows', 0...]
    another operation x0 -> x3, local copies, waits for them, and re-layouts: none -> 51 us  [the longest x2 44.2 us: on_device(): picked = jnp.take(whole.reshape(feat_loc, -1, tile_edge), flat_cols, axis=1)]
    all_gather x1, waiting for transfers between devices: 29.9 us -> 46.8 us  [on_device(): agg_all = lax.all_gather(aggregated, 'feat', axis=0, tiled=True)]
    unnamed x6 -> x5, waiting for transfers between devices: 49.5 us -> 49.1 us
  transfers between devices with their start and end apart: 5 -> 5, of which waited for: 5 -> 5; matrix products, arithmetic and copies ran while one was open for 9% -> 8% of each run, Pallas kernels for 0% -> 0%
where the time goes in v1:
time: 1570 us; the launch traced here: 1560 us
  waiting for transfers between devices  1220 us (78%)
  local copies, waits for them, and re-layouts  139 us (9%)
  other arithmetic  78.5 us (5%)
  blocking collectives  69.7 us (4%)
  matrix products  33.1 us (2%)
    reduce_scatter x1, waiting for transfers between devices, on_device(): lax.psum_scatter(terms.reshape(feat_loc, -1), 'rows', scatter_dimension=1...  724 us
    all_to_all x1, waiting for transfers between devices, on_device(): lax.all_to_all(jnp.stack([node_feats] * lax.axis_size('rows')), 'rows', 0...  340 us
    scatter-add x1, other arithmetic, on_device(): terms = jnp.zeros((feat_loc, row_devs * own_blocks, tile_edge), jnp.float...  78.5 us
    psum x1, blocking collectives, on_device(): grad_weight, grad_bias = lax.psum((weight_part, bias_part), 'rows')  69.7 us
    psum x1, waiting for transfers between devices, on_device(): grad_weight, grad_bias = lax.psum((weight_part, bias_part), 'rows')  61.2 us
    unnamed x5, waiting for transfers between devices  49.1 us
    all_gather x1, waiting for transfers between devices, on_device(): agg_all = lax.all_gather(aggregated, 'feat', axis=0, tiled=True)  46.8 us
    another operation x2, local copies, waits for them, and re-layouts, on_device(): picked = jnp.take(whole.reshape(feat_loc, -1, tile_edge), flat_cols, axis=1)  44.2 us
  transfers between devices with their start and end apart: 5, of which 5 were waited for; matrix products, arithmetic and copies ran while one was open for 8% of the time, Pallas kernels for 0%

profile of v1, /device:TPU:1, one launch (start us, length us, event | category | flops | bytes accessed | tf_op | source)
XLA Modules:
  0.0 1564.5 jit_solution(7439160054739187718)
XLA Ops:
  7.2 0.0 copy-start
  7.2 6.8 stack.2
  13.9 0.0 copy-start.3
  13.9 9.5 all-to-all-start
  23.4 0.0 all-gather.2.cloned.1.call-start
  23.5 0.0 copy-done.3
  23.5 0.1 copy.20
  23.6 0.1 copy.18
  23.7 0.1 reshape.66
  23.8 340.0 %all-to-all-done = bf16[32,64,4096]{2,1,0:T(8,128)(2,1)} async-done(((bf16[32,64,4096]{2,1,0:T(8,128)(2,1)}), bf16[32,64,4096]{2,1,0:T(8,128)(2,1)}, u32[]{:S(2)}, u32[]{:S(2)}) %all-to-all-start) | async-done | bytes 16777248 | tf_op jit(solution)/shard_map/all_to_all | solution.py:15
  363.8 18.5 %copy.19 = bf16[64,32,4096]{2,1,0:T(8,128)(2,1)} copy(bf16[64,32,4096]{2,0,1:T(8,128)(2,1)} %bitcast) | data formatting | bytes 33554432 | tf_op jit(solution)/shard_map/reshape | solution.py:14
  382.2 25.6 %reshape_reshape.3 = bf16[64,1024,128]{2,1,0:T(8,128)(2,1)} reshape(bf16[64,32,4096]{2,1,0:T(8,128)(2,1)} %copy.19) | data formatting | bytes 33554432 | tf_op jit(solution)/shard_map/reshape;reshape | solution.py:17
  407.9 18.6 %copy.21 = bf16[64,1024,128]{2,0,1:T(8,128)(2,1)} copy(bf16[64,1024,128]{2,1,0:T(8,128)(2,1)} %reshape_reshape.3) | data formatting | bytes 33554432 | tf_op jit(solution)/shard_map/reshape;reshape | solution.py:17
  426.5 25.4 %gather_fusion = bf16[512,64,128]{2,1,0:T(8,128)(2,1)} fusion(bf16[64,1024,128]{2,0,1:T(8,128)(2,1)} %copy.21, s32[1024]{0:T(1024)S(1)} %pad_clamp_fusion), kind=kCustom, calls=%fused_computation | custom fusion | bytes 16779264 | tf_op jit(solution)/shard_map/jit(_take)/gather | solution.py:17
  451.9 0.0 copy-start.4
  451.9 0.0 copy-start.5
  451.9 11.6 fusion.11
  463.5 0.9 copy.35
  464.4 0.0 all-gather.2.cloned.1.call-update
  464.4 0.0 reduce-scatter.7.cloned.1.call-start
  464.4 46.8 %all-gather.2.cloned.1.call-done = bf16[256,4096]{1,0:T(8,128)(2,1)} async-done(((bf16[64,4096]{1,0:T(8,128)(2,1)}), bf16[256,4096]{1,0:T(8,128)(2,1)}) %all-gather.2.cloned.1.call-update) | async-done | bytes 2097168 | tf_op jit(solution)/shard_map/all_gather | solution.py:21
  511.3 0.0 copy-done
  511.3 0.0 copy-done.4
  511.3 0.0 copy-done.5
  511.3 0.0 copy-start.2
  511.3 3.5 convert_reduce_fusion
  514.8 2.7 convolution_bitcast_fusion
  517.5 5.6 copy.29
  523.1 0.0 reduce-scatter.7.cloned.1.call-update
  523.2 0.0 all-reduce.2.cloned.1.call-start
  523.2 0.0 copy-done.2
  523.2 1.4 fusion.16
  524.6 0.0 all-reduce.2.cloned.1.call-update
  524.6 0.0 reduce-scatter.5.cloned.1.call-start
  524.7 49.0 %reduce-scatter.7.cloned.1.call-done = f32[64,4096]{1,0:T(8,128)} async-done(((f32[256,4096]{1,0:T(8,128)}), f32[64,4096]{1,0:T(8,128)}) %reduce-scatter.7.cloned.1.call-update) | async-done | bytes 1048592
  573.7 1.7 copy.30
  575.4 14.0 fusion.15
  589.3 11.3 broadcast_in_dim.17
  600.6 78.5 %scatter_fusion = f32[64,1024,128]{2,0,1:T(8,128)} fusion(f32[64,1024,128]{2,0,1:T(8,128)} %broadcast_in_dim.17, s32[512]{0:T(512)S(1)} %bitcast.52, f32[512,64,128]{2,1,0:T(8,128)} %bitcast.47), kind=kCustom, calls=%fused_computation.1 | custom fusion | flops 4194304 | bytes 50333696 | tf_op jit(solution)/shard_map/scatter-add | solution.py:55
  679.1 22.5 %copy_bitcast_fusion = f32[64,131072]{1,0:T(8,128)} fusion(f32[64,1024,128]{2,0,1:T(8,128)} %scatter_fusion), kind=kLoop, calls=%fused_computation.2 | loop fusion | bytes 67108864 | tf_op jit(solution)/shard_map/reshape | solution.py:58
  701.5 0.0 copy-start.1
  701.5 0.0 reduce-scatter.5.cloned.1.call-update
  701.6 69.7 %psum.15 = f32[64]{0:T(128)} all-reduce(f32[64]{0:T(128)S(1)} %get-tuple-element.4), channel_id=1, replica_groups=mesh['rows'=32,'feat'=4] {'rows'}, use_global_device_ids=true, to_apply=%region_5.6 | all-reduce | flops 64 | bytes 512 | tf_op jit(solution)/shard_map/psum | solution.py:37
  771.2 61.2 %all-reduce.2.cloned.1.call-done = f32[256,64]{0,1:T(8,128)} async-done(((f32[256,64]{0,1:T(8,128)}), f32[256,64]{0,1:T(8,128)}) %all-reduce.2.cloned.1.call-update) | async-done | bytes 65552 | tf_op jit(solution)/shard_map/psum | solution.py:37
  832.4 724.1 %reduce-scatter.5.cloned.1.call-done = f32[64,4096]{1,0:T(8,128)} async-done(((f32[64,131072]{1,0:T(8,128)}), f32[64,4096]{1,0:T(8,128)}) %reduce-scatter.5.cloned.1.call-update) | async-done | bytes 1048592 | tf_op jit(solution)/shard_map/reduce_scatter | solution.py:57
  1556.5 1.5 copy.38
  1558.0 0.0 copy-done.1
  (3 shorter events, 0.0 us)
Async XLA Ops:
  7.2 504.1 %copy-start = (bf16[256,64]{0,1:T(8,128)(2,1)S(1)}, bf16[256,64]{0,1:T(8,128)(2,1)}, u32[]{:S(2)}) copy-start(bf16[256,64]{0,1:T(8,128)(2,1)} %param.9) | copy-start | bytes 98308
  13.9 9.5 copy-start.3
  13.9 349.8 %all-to-all-start = ((bf16[32,64,4096]{2,1,0:T(8,128)(2,1)}), bf16[32,64,4096]{2,1,0:T(8,128)(2,1)}, u32[]{:S(2)}, u32[]{:S(2)}) async-start(bf16[32,64,4096]{2,1,0:T(8,128)(2,1)} %stack.2), calls=%async_computation | async-start | bytes 33554432 | tf_op jit(solution)/shard_map/all_to_all | solution.py:15
  23.4 487.9 %all-gather.2.cloned.1.call-start = ((), (), s32[]{:S(2)}) async-start(), calls=%async_computation.3 | async-start | bytes 2621440 | tf_op jit(solution)/shard_map/all_gather | solution.py:21
  451.9 59.4 %copy-start.4 = (bf16[64,4096]{1,0:T(8,128)(2,1)S(1)}, bf16[64,4096]{1,0:T(8,128)(2,1)}, u32[]{:S(2)}) copy-start(bf16[64,4096]{1,0:T(8,128)(2,1)} %param.11) | copy-start | bytes 1572868
  451.9 59.4 %copy-start.5 = (f32[64]{0:T(128)S(1)}, f32[64]{0:T(128)}, u32[]{:S(2)}) copy-start(f32[64]{0:T(128)} %param.10) | copy-start | bytes 772
  464.4 109.3 %reduce-scatter.7.cloned.1.call-start = ((), (), s32[]{:S(2)}) async-start(), calls=%async_computation.6 | async-start | bytes 5242880
  511.3 11.9 copy-start.2
  523.2 309.2 %all-reduce.2.cloned.1.call-start = ((), (), s32[]{:S(2)}) async-start(), calls=%async_computation.5 | async-start | bytes 131072 | tf_op jit(solution)/shard_map/psum | solution.py:37
  524.6 1031.9 %reduce-scatter.5.cloned.1.call-start = ((), (), s32[]{:S(2)}) async-start(), calls=%async_computation.4 | async-start | bytes 34603008 | tf_op jit(solution)/shard_map/reduce_scatter | solution.py:57
  701.5 856.5 %copy-start.1 = (bf16[256,64]{0,1:T(8,128)(2,1)S(1)}, bf16[256,64]{0,1:T(8,128)(2,1)}, u32[]{:S(2)}) copy-start(bf16[256,64]{0,1:T(8,128)(2,1)} %param.9) | copy-start | bytes 98308
Sparse Core Ops, SparseCore 0:
  464.5 46.7 all-gather.1
  523.3 50.3 reduce-scatter.6
  576.9 255.4 all-reduce.1
  835.2 721.2 reduce-scatter.4
